TPU v7x, 32 devices: a whole 2x2x4 slice. The times are simulated.
32 devices in a mesh: row: 16 (over z, y, core), col: 2 (over x).
Axes of the slice: x: 2, y: 2, z: 4, core: 2. Of those that a mesh axis runs over, the one named last changes fastest.
Arguments:
- node_features: float32 [4096, 128], P(('row', 'col')), may hold values from -6 to 6
- block_values: float32 [16, 2, 4, 128, 128], P('row', 'col')
- block_rows: int32 [16, 2, 4], P('row', 'col'), may hold values from 0 to 1, as said below
- block_cols: int32 [16, 2, 4], P('row', 'col'), may hold values from 0 to 15
- block_count: int32 [16, 2], P('row', 'col'), may hold values from 1 to 4, as said below
- w_input: float32 [128, 512], replicated, may hold values from -0.5 to 0.5
- bias_input: float32 [512], replicated, may hold values from -3 to 3
- gain_attn: float32 [512], replicated, may hold values from 0.1 to 1.9
- shift_attn: float32 [512], replicated, may hold values from -3 to 3
- w_heads: float32 [512, 1536], replicated, may hold values from -0.25 to 0.25
- w_merge: float32 [512, 512], replicated, may hold values from -0.75 to 0.75
- bias_merge: float32 [512], replicated, may hold values from -3 to 3
- gain_ffn: float32 [512], replicated, may hold values from 0.1 to 1.9
- shift_ffn: float32 [512], replicated, may hold values from -3 to 3
- w_expand: float32 [512, 1024], replicated, may hold values from -0.25 to 0.25
- bias_expand: float32 [1024], replicated, may hold values from -3 to 3
- w_reduce: float32 [1024, 512], replicated, may hold values from -0.25 to 0.25
- bias_reduce: float32 [512], replicated, may hold values from -3 to 3
- readout: float32 [512], replicated, may hold values from -0.25 to 0.25
- cotangent: float32 [4096, 512], P(('row', 'col')), may hold values from -6 to 6
Outputs:
- layer_out: float32 [4096, 512], P(('row', 'col'))
- grad_features: float32 [4096, 128], P(('row', 'col'))
- grad_w_input: float32 [128, 512], replicated
- grad_bias_input: float32 [512], replicated
- grad_gain_attn: float32 [512], replicated
- grad_shift_attn: float32 [512], replicated
- grad_w_heads: float32 [512, 1536], replicated
- grad_w_merge: float32 [512, 512], replicated
- grad_bias_merge: float32 [512], replicated
- grad_gain_ffn: float32 [512], replicated
- grad_shift_ffn: float32 [512], replicated
- grad_w_expand: float32 [512, 1024], replicated
- grad_bias_expand: float32 [1024], replicated
- grad_w_reduce: float32 [1024, 512], replicated
- grad_bias_reduce: float32 [512], replicated
- grad_readout: float32 [512], replicated
Inputs may be any that keep to these rules, and one draw needn't show every extreme that they name: Within one tile the listed (block_rows, block_cols) pairs are all different. Slots 0 to block_count - 1 of a tile are live, the rest are ignored; some tile has all 4 slots live.
All inputs are finite; a program needn't handle non-finite values.
Results may differ from a plain program's by a relative error of at most 0.0003.
Values sent between devices are 32-bit elements; how exact they have to be, the bound alone decides.
No kernel may reach another device: no remote copies, remote signals or barrier semaphores. Data moves between devices by JAX's collectives and lax.ppermute only.
A program may use at most 192 MiB of HBM per device.

v0:
```python
import math
import jax
import jax.numpy as jnp
from jax import lax
from jax.sharding import PartitionSpec as P

HEADS = 8
HEAD_DIM = 64
HOPS = 7
exact = lax.Precision.HIGHEST


def layer_norm(values, gain, shift):
    average = jnp.mean(values, axis=-1, keepdims=True)
    centred = values - average
    spread = jnp.mean(centred * centred, axis=-1, keepdims=True)
    return centred * lax.rsqrt(spread + 1e-05) * gain + shift


def node_tail(
    start,
    gain_attn,
    shift_attn,
    w_heads,
    w_merge,
    bias_merge,
    gain_ffn,
    shift_ffn,
    w_expand,
    bias_expand,
    w_reduce,
    bias_reduce,
    readout,
):
    node_count, token_count, columns = start.shape
    normed = layer_norm(start, gain_attn, shift_attn)
    projected = jnp.einsum("ntd,de->nte", normed, w_heads, precision=exact)
    queries = projected[..., :columns].reshape(node_count, token_count, HEADS, HEAD_DIM)
    key_rows = projected[..., columns : 2 * columns].reshape(
        node_count, token_count, HEADS, HEAD_DIM
    )
    value_rows = projected[..., 2 * columns :].reshape(node_count, token_count, HEADS, HEAD_DIM)
    scores = jnp.einsum("nqhe,nkhe->nhqk", queries, key_rows, precision=exact) / math.sqrt(HEAD_DIM)
    attention = jax.nn.softmax(scores, axis=-1)
    mixed = jnp.einsum("nhqk,nkhe->nqhe", attention, value_rows, precision=exact).reshape(
        node_count, token_count, columns
    )
    middle = start + jnp.einsum("ntd,de->nte", mixed, w_merge, precision=exact) + bias_merge
    normed_two = layer_norm(middle, gain_ffn, shift_ffn)
    activated = jax.nn.gelu(
        jnp.einsum("ntd,de->nte", normed_two, w_expand, precision=exact) + bias_expand,
        approximate=False,
    )
    final = middle + jnp.einsum("nte,ed->ntd", activated, w_reduce, precision=exact) + bias_reduce
    center = final[:, 0]
    others = final[:, 1:]
    weights = jax.nn.softmax(jnp.einsum("nkd,d->nk", others, readout, precision=exact), axis=-1)
    return center + jnp.einsum("nk,nkd->nd", weights, others, precision=exact)


def per_device(
    node_features,
    block_values,
    block_rows,
    block_cols,
    block_count,
    w_input,
    bias_input,
    gain_attn,
    shift_attn,
    w_heads,
    w_merge,
    bias_merge,
    gain_ffn,
    shift_ffn,
    w_expand,
    bias_expand,
    w_reduce,
    bias_reduce,
    readout,
    cotangent,
):
    values = block_values[0, 0]
    row_ids = block_rows[0, 0]
    col_ids = block_cols[0, 0]
    block_size = values.shape[-1]
    node_count = node_features.shape[0]
    row_blocks = lax.axis_size("col") * node_count // block_size
    col_blocks = lax.axis_size("row") * node_count // block_size
    is_live = (jnp.arange(values.shape[0]) < block_count[0, 0]).astype(jnp.float32)
    row_table = (row_ids[:, None] == jnp.arange(row_blocks)[None, :]).astype(jnp.float32) * is_live[
        :, None
    ]
    col_table = (col_ids[:, None] == jnp.arange(col_blocks)[None, :]).astype(jnp.float32) * is_live[
        :, None
    ]
    hop_list = [node_features]
    for hop_index in range(HOPS):
        field = hop_list[-1]
        forward_columns = field.shape[1]
        forward_gathered = lax.all_gather(field, "row", axis=0, tiled=True).reshape(
            col_blocks, block_size, forward_columns
        )
        forward_picked = forward_gathered[col_ids]
        forward_products = jnp.einsum("bij,bjw->biw", values, forward_picked, precision=exact)
        forward_partial_value = jnp.einsum(
            "br,biw->riw", row_table, forward_products, precision=exact
        ).reshape(row_blocks * block_size, forward_columns)
        hop_list.append(
            lax.psum_scatter(forward_partial_value, "col", scatter_dimension=0, tiled=True)
        )
    stacked = jnp.stack(hop_list, axis=1)

    def local_layer(
        stacked_hops,
        w_input,
        bias_input,
        gain_attn,
        shift_attn,
        w_heads,
        w_merge,
        bias_merge,
        gain_ffn,
        shift_ffn,
        w_expand,
        bias_expand,
        w_reduce,
        bias_reduce,
        readout,
    ):
        start = jnp.einsum("ntf,fd->ntd", stacked_hops, w_input, precision=exact) + bias_input
        return node_tail(
            start,
            gain_attn,
            shift_attn,
            w_heads,
            w_merge,
            bias_merge,
            gain_ffn,
            shift_ffn,
            w_expand,
            bias_expand,
            w_reduce,
            bias_reduce,
            readout,
        )

    layer_out, pullback = jax.vjp(
        local_layer,
        stacked,
        w_input,
        bias_input,
        gain_attn,
        shift_attn,
        w_heads,
        w_merge,
        bias_merge,
        gain_ffn,
        shift_ffn,
        w_expand,
        bias_expand,
        w_reduce,
        bias_reduce,
        readout,
    )
    (
        grad_hops,
        grad_w_input,
        grad_bias_input,
        grad_gain_attn,
        grad_shift_attn,
        grad_w_heads,
        grad_w_merge,
        grad_bias_merge,
        grad_gain_ffn,
        grad_shift_ffn,
        grad_w_expand,
        grad_bias_expand,
        grad_w_reduce,
        grad_bias_reduce,
        grad_readout,
    ) = pullback(cotangent)
    carried = grad_hops[:, HOPS]
    for hop_index in range(HOPS - 1, -1, -1):
        columns = carried.shape[1]
        gathered = lax.all_gather(carried, "col", axis=0, tiled=True).reshape(
            row_blocks, block_size, columns
        )
        picked = gathered[row_ids]
        products = jnp.einsum("bji,bjw->biw", values, picked, precision=exact)
        partial_value = jnp.einsum("bc,biw->ciw", col_table, products, precision=exact).reshape(
            col_blocks * block_size, columns
        )
        carried = grad_hops[:, hop_index] + lax.psum_scatter(
            partial_value, "row", scatter_dimension=0, tiled=True
        )
    summed = lax.psum(
        (
            grad_w_input,
            grad_bias_input,
            grad_gain_attn,
            grad_shift_attn,
            grad_w_heads,
            grad_w_merge,
            grad_bias_merge,
            grad_gain_ffn,
            grad_shift_ffn,
            grad_w_expand,
            grad_bias_expand,
            grad_w_reduce,
            grad_bias_reduce,
            grad_readout,
        ),
        ("row", "col"),
    )
    return (
        layer_out,
        carried,
        summed[0],
        summed[1],
        summed[2],
        summed[3],
        summed[4],
        summed[5],
        summed[6],
        summed[7],
        summed[8],
        summed[9],
        summed[10],
        summed[11],
        summed[12],
        summed[13],
    )


def solution(mesh):
    placed = (
        P(("row", "col"), None),
        P("row", "col", None, None, None),
        P("row", "col", None),
        P("row", "col", None),
        P("row", "col"),
        P(),
        P(),
        P(),
        P(),
        P(),
        P(),
        P(),
        P(),
        P(),
        P(),
        P(),
        P(),
        P(),
        P(),
        P(("row", "col"), None),
    )
    return jax.shard_map(
        per_device,
        mesh=mesh,
        in_specs=placed,
        out_specs=(
            P(("row", "col"), None),
            P(("row", "col"), None),
            P(),
            P(),
            P(),
            P(),
            P(),
            P(),
            P(),
            P(),
            P(),
            P(),
            P(),
            P(),
            P(),
            P(),
        ),
        check_vma=False,
    )
```

profile of v0, /device:TPU:0, one launch (start us, length us, event | category | flops | bytes accessed | tf_op | source)
XLA Modules:
  0.0 1398.2 jit_solution(17185425207712821760)
XLA Ops:
  9.5 41.4 %all-gather.9.cloned.1.call-done = f32[2048,128]{1,0:T(8,128)} async-done(((f32[128,128]{1,0:T(8,128)}), f32[2048,128]{1,0:T(8,128)}) %all-gather.9.cloned.1.call-update) | async-done | bytes 1048592 | tf_op jit(solution)/shard_map/all_gather | solution.py:101
  59.8 9.3 reduce-scatter.15.cloned.1.call-done
  69.1 40.1 %all-gather.11.cloned.1.call-done = f32[2048,128]{1,0:T(8,128)} async-done(((f32[128,128]{1,0:T(8,128)}), f32[2048,128]{1,0:T(8,128)}) %all-gather.11.cloned.1.call-update) | async-done | bytes 1048592 | tf_op jit(solution)/shard_map/all_gather | solution.py:101
  118.1 9.3 reduce-scatter.17.cloned.1.call-done
  127.4 39.9 %all-gather.13.cloned.1.call-done = f32[2048,128]{1,0:T(8,128)} async-done(((f32[128,128]{1,0:T(8,128)}), f32[2048,128]{1,0:T(8,128)}) %all-gather.13.cloned.1.call-update) | async-done | bytes 1048592 | tf_op jit(solution)/shard_map/all_gather | solution.py:101
  176.1 9.3 reduce-scatter.19.cloned.1.call-done
  185.4 40.1 %all-gather.15.cloned.1.call-done = f32[2048,128]{1,0:T(8,128)} async-done(((f32[128,128]{1,0:T(8,128)}), f32[2048,128]{1,0:T(8,128)}) %all-gather.15.cloned.1.call-update) | async-done | bytes 1048592 | tf_op jit(solution)/shard_map/all_gather | solution.py:101
  234.3 9.3 reduce-scatter.21.cloned.1.call-done
  243.7 40.1 %all-gather.17.cloned.1.call-done = f32[2048,128]{1,0:T(8,128)} async-done(((f32[128,128]{1,0:T(8,128)}), f32[2048,128]{1,0:T(8,128)}) %all-gather.17.cloned.1.call-update) | async-done | bytes 1048592 | tf_op jit(solution)/shard_map/all_gather | solution.py:101
  292.5 9.3 reduce-scatter.23.cloned.1.call-done
  301.9 40.1 %all-gather.19.cloned.1.call-done = f32[2048,128]{1,0:T(8,128)} async-done(((f32[128,128]{1,0:T(8,128)}), f32[2048,128]{1,0:T(8,128)}) %all-gather.19.cloned.1.call-update) | async-done | bytes 1048592 | tf_op jit(solution)/shard_map/all_gather | solution.py:101
  350.7 9.3 reduce-scatter.25.cloned.1.call-done
  366.4 33.8 %all-gather.21.cloned.1.call-done = f32[2048,128]{1,0:T(8,128)} async-done(((f32[128,128]{1,0:T(8,128)}), f32[2048,128]{1,0:T(8,128)}) %all-gather.21.cloned.1.call-update) | async-done | bytes 1048592 | tf_op jit(solution)/shard_map/all_gather | solution.py:101
  412.1 6.1 reduce-scatter.27.cloned.1.call-done
  424.0 10.8 fusion.10
  434.9 14.4 %fusion.197 = (f32[128,8,512]{2,0,1:T(8,128)}, f32[128,8,512]{2,0,1:T(8,128)}, f32[128,8,512]{2,0,1:T(8,128)}) fusion(f32[128,8,1536]{2,0,1:T(8,128)S(1)} %fusion.10), kind=kLoop, calls=%fused_computation.285 | loop fusion | bytes 12582912 | tf_op jit(solution)/shard_map/jvp()/slice | solution.py:39
  452.2 5.6 copy.68
  460.7 5.6 copy.67
  469.2 5.6 copy.69
  474.8 9.8 multiply_reduce_fusion.1
  488.8 10.2 convolution_bitcast_fusion.3
  499.0 5.1 copy.71
  504.2 6.4 fusion.198
  511.1 8.1 fusion.47
  519.2 9.3 fusion.2
  528.6 7.0 add_add_fusion.4
  541.2 6.7 fusion.12
  549.4 14.6 %fusion.199 = (f32[1024]{0:T(1024)}, f32[128,8,1024]{2,0,1:T(8,128)S(1)}) fusion(f32[128,8,1024]{2,0,1:T(8,128)} %copy-done.9, f32[1024,512]{1,0:T(8,128)} %param.36, f32[128,1,512]{2,0,1:T(8,128)} %bitcast.328, f32[128,7,512]{2,0,1:T(8,128)S(1)} %multiply_add_fusion.3, f32[128,8,1024]{2,0,1:T(8,128)} %copy-done.7, f32[1024]{0:T(1024)S(1)} %copy-done.43), kind=kOutput, calls=%fused_computation.287 | convolution fusion | flops 6458702848 | bytes 16785408 | tf_op jit(solution)/shard_map/transpose(jvp(nte,ed->ntd))/dot_general | solution.py:54
  564.0 7.7 fusion.193
  581.2 5.8 copy.74
  587.0 16.1 %multiply_reduce_fusion = (f32[128,8,8]{2,1,0:T(8,128)}, f32[128,8,8,8]{2,3,1,0:T(8,128)}) fusion(f32[128,8,8]{2,1,0:T(8,128)} %multiply_divide_fusion, f32[128,8,8]{2,1,0:T(8,128)} %copy-done.20, f32[128,8,8,8]{2,3,1,0:T(8,128)} %copy-done.10, f32[128,8,64,8]{2,3,1,0:T(8,128)} %copy.74, f32[128,8,8,64]{3,1,2,0:T(8,128)} %copy.69), kind=kOutput, calls=%fused_computation.25 | convolution fusion | flops 50651136 | bytes 4816896 | tf_op jit(solution)/shard_map/transpose(jvp(nhqk,nkhe->nqhe))/dot_general | solution.py:45
  605.0 12.5 convolution_bitcast_fusion
  617.5 14.7 %convolution_bitcast_fusion.1 = f32[128,8,8,64]{3,1,2,0:T(8,128)} fusion(f32[128,8,8,64]{3,1,2,0:T(8,128)} %copy.67, f32[128,8,8,8]{2,3,1,0:T(8,128)} %get-tuple-element.59, f32[128,8,8]{2,1,0:T(8,128)} %copy-done.39, f32[128,8,8]{2,1,0:T(8,128)S(1)} %copy-done.30, f32[128,8,8]{2,1,0:T(8,128)S(1)} %copy-done.21, f32[128,8,8,8]{2,3,1,0:T(8,128)} %copy-done.10), kind=kOutput, calls=%fused_computation.49 | convolution fusion | flops 50724864 | bytes 4816896 | tf_op jit(solution)/shard_map/transpose(jvp(nqhe,nkhe->nhqk))/dot_general | solution.py:43
  632.2 13.5 convolution_bitcast_fusion.2
  659.9 24.2 %fusion.194 = (f32[512]{0:T(512)}, f32[128,8]{0,1:T(8,128)S(1)}, f32[128,8,512]{2,0,1:T(8,128)S(1)}) fusion(f32[512]{0:T(512)S(1)} %copy-done.55, f32[128,8]{0,1:T(8,128)S(1)} %broadcast_multiply_fusion.1, f32[128,8,512]{2,0,1:T(8,128)} %copy-done.3, f32[512]{0:T(512)S(1)} %copy-done.42, f32[512,1536]{1,0:T(8,128)S(1)} %copy-done, ...), kind=kOutput, calls=%fused_computation.282 | convolution fusion | flops 9669965824 | bytes 13645824 | tf_op jit(solution)/shard_map/transpose(jvp(ntd,de->nte))/dot_general | solution.py:37
  705.3 57.6 %reduce-scatter.29.cloned.1.call-done = f32[128,128]{1,0:T(8,128)} async-done(((f32[2048,128]{1,0:T(8,128)}), f32[128,128]{1,0:T(8,128)}) %reduce-scatter.29.cloned.1.call-update) | async-done | bytes 65552 | tf_op jit(solution)/shard_map/reduce_scatter | solution.py:194
  777.6 56.5 %reduce-scatter.31.cloned.1.call-done = f32[128,128]{1,0:T(8,128)} async-done(((f32[2048,128]{1,0:T(8,128)}), f32[128,128]{1,0:T(8,128)}) %reduce-scatter.31.cloned.1.call-update) | async-done | bytes 65552 | tf_op jit(solution)/shard_map/reduce_scatter | solution.py:194
  848.9 56.5 %reduce-scatter.33.cloned.1.call-done = f32[128,128]{1,0:T(8,128)} async-done(((f32[2048,128]{1,0:T(8,128)}), f32[128,128]{1,0:T(8,128)}) %reduce-scatter.33.cloned.1.call-update) | async-done | bytes 65552 | tf_op jit(solution)/shard_map/reduce_scatter | solution.py:194
  920.1 56.5 %reduce-scatter.35.cloned.1.call-done = f32[128,128]{1,0:T(8,128)} async-done(((f32[2048,128]{1,0:T(8,128)}), f32[128,128]{1,0:T(8,128)}) %reduce-scatter.35.cloned.1.call-update) | async-done | bytes 65552 | tf_op jit(solution)/shard_map/reduce_scatter | solution.py:194
  977.5 5.3 all_gather.53
  991.8 56.4 %reduce-scatter.37.cloned.1.call-done = f32[128,128]{1,0:T(8,128)} async-done(((f32[2048,128]{1,0:T(8,128)}), f32[128,128]{1,0:T(8,128)}) %reduce-scatter.37.cloned.1.call-update) | async-done | bytes 65552 | tf_op jit(solution)/shard_map/reduce_scatter | solution.py:194
  1062.9 11.2 fusion.24
  1074.1 45.4 %reduce-scatter.39.cloned.1.call-done = f32[128,128]{1,0:T(8,128)} async-done(((f32[2048,128]{1,0:T(8,128)}), f32[128,128]{1,0:T(8,128)}) %reduce-scatter.39.cloned.1.call-update) | async-done | bytes 65552 | tf_op jit(solution)/shard_map/reduce_scatter | solution.py:194
  1137.5 6.8 convolution_bitcast_fusion.5
  1144.3 10.2 convolution_bitcast_fusion.4
  1154.7 22.1 %fusion.8 = f32[512,1536]{1,0:T(8,128)} fusion(f32[128,8,512]{0,2,1:T(8,128)S(1)} %bitcast.343, f32[128,8,512]{0,2,1:T(8,128)S(1)} %bitcast.341, f32[128,8,512]{0,2,1:T(8,128)S(1)} %bitcast.339, f32[512]{0:T(512)S(1)} %copy-done.69, f32[512]{0:T(512)S(1)} %copy-done.56, f32[128,8]{0,1:T(8,128)S(1)} %copy-done.46, f32[128,8,512]{2,0,1:T(8,128)S(1)} %copy-done.5, ...), kind=kOutput, calls=%fused_computation.42 | convolution fusion | flops 9669443584 | bytes 11548672 | tf_op jit(solution)/shard_map/transpose(jvp(ntd,de->nte))/dot_general | solution.py:37
  1180.1 41.8 %all-reduce.5 = (f32[512]{0:T(512)}, f32[512]{0:T(512)}, f32[512]{0:T(512)}, f32[512]{0:T(512)}, f32[512]{0:T(512)}, /*index=5*/f32[512]{0:T(512)}, f32[1024]{0:T(1024)}, f32[512]{0:T(512)}, f32[512]{0:T(512)}) all-reduce(f32[512]{0:T(512)S(1)} %copy-done.60, f32[512]{0:T(512)S(1)} %copy-done.59, ...), channel_id=1, replica_groups=mesh['row'=16,'col'=2] {'row','col'}, use_global_device_ids=true, to_apply=%region_30.0 | all-reduce | flops 5120 | bytes 40960 | tf_op jit(solution)/shard_map/psum | solution.py:197
  1229.5 152.0 %all-reduce.9.cloned.1.call-done = (f32[128,512]{1,0:T(8,128)}, f32[512,1536]{1,0:T(8,128)}, f32[512,512]{1,0:T(8,128)}, f32[512,1024]{1,0:T(8,128)}, f32[1024,512]{1,0:T(8,128)}) async-done(((f32[128,512]{1,0:T(8,128)}, f32[512,1536]{1,0:T(8,128)}, f32[512,512]{1,0:T(8,128)}, f32[512,1024]{1,0:T(8,128)}, f32[1024,512]{1,0:T(8,128)}), (f32[128,512]{1,0:T(8,128)}, f32[512,1536]{1,0:T(8,128)}, ...) | async-done | bytes 8650768 | tf_op jit(solution)/shard_map/psum | solution.py:197
  (329 shorter events, 252.2 us)
Async XLA Ops:
  7.2 416.8 %copy-start = (f32[512,1536]{1,0:T(8,128)S(1)}, f32[512,1536]{1,0:T(8,128)}, u32[]{:S(2)}) copy-start(f32[512,1536]{1,0:T(8,128)} %param.29) | copy-start | bytes 9437188
  7.2 162.6 %copy-start.6 = (f32[1,1,4,128,128]{4,3,2,1,0:T(8,128)S(1)}, f32[1,1,4,128,128]{4,3,2,1,0:T(8,128)}, u32[]{:S(2)}) copy-start(f32[1,1,4,128,128]{4,3,2,1,0:T(8,128)} %param.21) | copy-start | bytes 786436
  7.2 108.6 %copy-start.52 = (s32[1,1,4]{2,1,0:T(1,128)S(1)}, s32[1,1,4]{2,1,0:T(1,128)}, u32[]{:S(2)}) copy-start(s32[1,1,4]{2,1,0:T(1,128)} %param.22) | copy-start | bytes 52
  7.2 43.7 %all-gather.9.cloned.1.call-start = ((), (), s32[]{:S(2)}) async-start(), calls=%async_computation.14 | async-start | bytes 1114112 | tf_op jit(solution)/shard_map/all_gather | solution.py:101
  8.0 61.1 %reduce-scatter.15.cloned.1.call-start = ((), (), s32[]{:S(2)}) async-start(), calls=%async_computation.15 | async-start | bytes 196608 | tf_op jit(solution)/shard_map/reduce_scatter | solution.py:110
  59.7 49.5 %all-gather.11.cloned.1.call-start = ((), (), s32[]{:S(2)}) async-start(), calls=%async_computation.16 | async-start | bytes 1114112 | tf_op jit(solution)/shard_map/all_gather | solution.py:101
  69.1 58.3 %reduce-scatter.17.cloned.1.call-start = ((), (), s32[]{:S(2)}) async-start(), calls=%async_computation.17 | async-start | bytes 196608 | tf_op jit(solution)/shard_map/reduce_scatter | solution.py:110
  118.0 49.3 %all-gather.13.cloned.1.call-start = ((), (), s32[]{:S(2)}) async-start(), calls=%async_computation.18 | async-start | bytes 1114112 | tf_op jit(solution)/shard_map/all_gather | solution.py:101
  127.3 58.0 %reduce-scatter.19.cloned.1.call-start = ((), (), s32[]{:S(2)}) async-start(), calls=%async_computation.19 | async-start | bytes 196608 | tf_op jit(solution)/shard_map/reduce_scatter | solution.py:110
  176.0 184.7 %copy-start.40 = (f32[128,128]{1,0:T(8,128)S(1)}, f32[128,128]{1,0:T(8,128)}, u32[]{:S(2)}) copy-start(f32[128,128]{1,0:T(8,128)} %param.20) | copy-start | bytes 196612
  176.0 185.3 %copy-start.41 = (f32[128,128]{1,0:T(8,128)S(1)}, f32[128,128]{1,0:T(8,128)}, u32[]{:S(2)}) copy-start(f32[128,128]{1,0:T(8,128)} %reduce-scatter.15.cloned.1.call-done) | copy-start | bytes 196612
  176.1 49.5 %all-gather.15.cloned.1.call-start = ((), (), s32[]{:S(2)}) async-start(), calls=%async_computation.20 | async-start | bytes 1114112 | tf_op jit(solution)/shard_map/all_gather | solution.py:101
  185.4 58.2 %reduce-scatter.21.cloned.1.call-start = ((), (), s32[]{:S(2)}) async-start(), calls=%async_computation.21 | async-start | bytes 196608 | tf_op jit(solution)/shard_map/reduce_scatter | solution.py:110
  234.3 49.5 %all-gather.17.cloned.1.call-start = ((), (), s32[]{:S(2)}) async-start(), calls=%async_computation.22 | async-start | bytes 1114112 | tf_op jit(solution)/shard_map/all_gather | solution.py:101
  243.6 58.2 %reduce-scatter.23.cloned.1.call-start = ((), (), s32[]{:S(2)}) async-start(), calls=%async_computation.23 | async-start | bytes 196608 | tf_op jit(solution)/shard_map/reduce_scatter | solution.py:110
  286.2 133.5 %copy-start.42 = (f32[512]{0:T(512)S(1)}, f32[512]{0:T(512)}, u32[]{:S(2)}) copy-start(f32[512]{0:T(512)} %param.26) | copy-start | bytes 6148
  292.5 49.5 %all-gather.19.cloned.1.call-start = ((), (), s32[]{:S(2)}) async-start(), calls=%async_computation.24 | async-start | bytes 1114112 | tf_op jit(solution)/shard_map/all_gather | solution.py:101
  301.8 58.2 %reduce-scatter.25.cloned.1.call-start = ((), (), s32[]{:S(2)}) async-start(), calls=%async_computation.25 | async-start | bytes 196608 | tf_op jit(solution)/shard_map/reduce_scatter | solution.py:110
  350.7 49.5 %all-gather.21.cloned.1.call-start = ((), (), s32[]{:S(2)}) async-start(), calls=%async_computation.26 | async-start | bytes 1114112 | tf_op jit(solution)/shard_map/all_gather | solution.py:101
  360.0 58.2 %reduce-scatter.27.cloned.1.call-start = ((), (), s32[]{:S(2)}) async-start(), calls=%async_computation.27 | async-start | bytes 196608 | tf_op jit(solution)/shard_map/reduce_scatter | solution.py:110
  361.9 62.1 %copy-start.55 = (f32[512]{0:T(512)S(1)}, f32[512]{0:T(512)}, u32[]{:S(2)}) copy-start(f32[512]{0:T(512)} %param.27) | copy-start | bytes 6148
  361.9 62.1 %copy-start.68 = (f32[512]{0:T(512)S(1)}, f32[512]{0:T(512)}, u32[]{:S(2)}) copy-start(f32[512]{0:T(512)} %param.28) | copy-start | bytes 6148
  408.9 354.0 %reduce-scatter.29.cloned.1.call-start = ((), (), s32[]{:S(2)}) async-start(), calls=%async_computation.28 | async-start | bytes 1114112 | tf_op jit(solution)/shard_map/reduce_scatter | solution.py:194
  424.0 262.0 %copy-start.45 = (f32[128,8]{0,1:T(8,128)}, f32[128,8]{0,1:T(8,128)S(1)}, u32[]{:S(2)}) copy-start(f32[128,8]{0,1:T(8,128)S(1)} %fusion.126) | copy-start | bytes 12292
  510.6 17.9 %copy-start.1 = (f32[128,8,512]{2,0,1:T(8,128)}, f32[128,8,512]{2,0,1:T(8,128)S(1)}, u32[]{:S(2)}) copy-start(f32[128,8,512]{2,0,1:T(8,128)S(1)} %get-tuple-element.55) | copy-start | bytes 6291460
  511.1 62.3 %copy-start.47 = (f32[128,8]{0,1:T(8,128)}, f32[128,8]{0,1:T(8,128)S(1)}, u32[]{:S(2)}) copy-start(f32[128,8]{0,1:T(8,128)S(1)} %fusion.127) | copy-start | bytes 12292
  548.0 15.9 %copy-start.48 = (f32[128,7]{0,1:T(8,128)}, f32[128,7]{0,1:T(8,128)S(1)}, u32[]{:S(2)}) copy-start(f32[128,7]{0,1:T(8,128)S(1)} %get-tuple-element.49) | copy-start | bytes 10756
  548.1 15.9 %copy-start.50 = (f32[128,7]{0,1:T(8,128)}, f32[128,7]{0,1:T(8,128)S(1)}, u32[]{:S(2)}) copy-start(f32[128,7]{0,1:T(8,128)S(1)} %get-tuple-element.48) | copy-start | bytes 10756
  549.3 24.1 %copy-start.18 = (f32[128,7,512]{2,0,1:T(8,128)}, f32[128,7,512]{2,0,1:T(8,128)S(1)}, u32[]{:S(2)}) copy-start(f32[128,7,512]{2,0,1:T(8,128)S(1)} %multiply_add_fusion.3) | copy-start | bytes 5505028
  549.3 14.7 %copy-start.2 = (f32[128,8,512]{2,0,1:T(8,128)S(1)}, f32[128,8,512]{2,0,1:T(8,128)}, u32[]{:S(2)}) copy-start(f32[128,8,512]{2,0,1:T(8,128)} %copy-done.1) | copy-start | bytes 6291460
  549.3 14.6 %copy-start.36 = (f32[512,1024]{1,0:T(8,128)S(1)}, f32[512,1024]{1,0:T(8,128)}, u32[]{:S(2)}) copy-start(f32[512,1024]{1,0:T(8,128)} %param.34) | copy-start | bytes 6291460
  587.0 18.0 %copy-start.11 = (f32[128,8,8,8]{2,3,1,0:T(8,128)S(1)}, f32[128,8,8,8]{2,3,1,0:T(8,128)}, u32[]{:S(2)}) copy-start(f32[128,8,8,8]{2,3,1,0:T(8,128)} %copy-done.10) | copy-start | bytes 786436
  587.0 18.0 %copy-start.16 = (f32[128,8,8,64]{3,1,2,0:T(8,128)S(1)}, f32[128,8,8,64]{3,1,2,0:T(8,128)}, u32[]{:S(2)}) copy-start(f32[128,8,8,64]{3,1,2,0:T(8,128)} %copy.68) | copy-start | bytes 6291460
  587.0 18.0 %copy-start.21 = (f32[128,8,8]{2,1,0:T(8,128)S(1)}, f32[128,8,8]{2,1,0:T(8,128)}, u32[]{:S(2)}) copy-start(f32[128,8,8]{2,1,0:T(8,128)} %copy-done.20) | copy-start | bytes 98308
  587.0 18.0 %copy-start.30 = (f32[128,8,8]{2,1,0:T(8,128)S(1)}, f32[128,8,8]{2,1,0:T(8,128)}, u32[]{:S(2)}) copy-start(f32[128,8,8]{2,1,0:T(8,128)} %copy-done.29) | copy-start | bytes 98308
  659.9 24.3 %copy-start.4 = (f32[128,8,512]{2,0,1:T(8,128)S(1)}, f32[128,8,512]{2,0,1:T(8,128)}, u32[]{:S(2)}) copy-start(f32[128,8,512]{2,0,1:T(8,128)} %copy-done.3) | copy-start | bytes 6291460
  705.3 128.9 %reduce-scatter.31.cloned.1.call-start = ((), (), s32[]{:S(2)}) async-start(), calls=%async_computation.29 | async-start | bytes 1114112 | tf_op jit(solution)/shard_map/reduce_scatter | solution.py:194
  777.6 127.8 %reduce-scatter.33.cloned.1.call-start = ((), (), s32[]{:S(2)}) async-start(), calls=%async_computation.30 | async-start | bytes 1114112 | tf_op jit(solution)/shard_map/reduce_scatter | solution.py:194
  848.8 127.8 %reduce-scatter.35.cloned.1.call-start = ((), (), s32[]{:S(2)}) async-start(), calls=%async_computation.31 | async-start | bytes 1114112 | tf_op jit(solution)/shard_map/reduce_scatter | solution.py:194
  920.1 128.1 %reduce-scatter.37.cloned.1.call-start = ((), (), s32[]{:S(2)}) async-start(), calls=%async_computation.32 | async-start | bytes 1114112 | tf_op jit(solution)/shard_map/reduce_scatter | solution.py:194
  991.7 127.8 %reduce-scatter.39.cloned.1.call-start = ((), (), s32[]{:S(2)}) async-start(), calls=%async_computation.33 | async-start | bytes 1114112 | tf_op jit(solution)/shard_map/reduce_scatter | solution.py:194
  1062.9 165.1 %reduce-scatter.41.cloned.1.call-start = ((), (), s32[]{:S(2)}) async-start(), calls=%async_computation.34 | async-start | bytes 1114112 | tf_op jit(solution)/shard_map/reduce_scatter | solution.py:194
  1133.2 11.0 copy-start.23
  1133.2 11.0 copy-start.44
  1133.2 248.3 %all-reduce.9.cloned.1.call-start = ((), (), s32[]{:S(2)}) async-start(), calls=%async_computation.35 | async-start | bytes 17301504 | tf_op jit(solution)/shard_map/psum | solution.py:197
  1133.5 10.8 copy-start.8
  1133.5 10.8 copy-start.19
  1144.3 10.3 copy-start.5
  (44 other events, 214.5 us)
Sparse Core Ops, SparseCore 0:
  10.2 40.6 all-gather.8
  59.8 9.1 reduce-scatter.14
  71.2 37.9 all-gather.10
  118.1 9.1 reduce-scatter.16
  129.3 37.9 all-gather.12
  176.2 9.1 reduce-scatter.18
  187.5 37.9 all-gather.14
  234.4 9.1 reduce-scatter.20
  245.7 37.9 all-gather.16
  292.6 9.1 reduce-scatter.22
  304.0 37.9 all-gather.18
  350.8 9.1 reduce-scatter.24
  362.2 37.9 all-gather.20
  409.0 9.1 reduce-scatter.26
  705.4 57.4 reduce-scatter.28
  777.7 56.4 reduce-scatter.30
  849.0 56.3 reduce-scatter.32
  920.2 56.4 reduce-scatter.34
  991.9 56.2 reduce-scatter.36
  1063.0 56.4 reduce-scatter.38
  1133.3 56.4 reduce-scatter.40
  1198.5 183.0 all-reduce.8
where the time goes:
time: 1410 us; the launch traced here: 1400 us
  waiting for transfers between devices  819 us (58%)
  matrix products  292 us (21%)
  local copies, waits for them, and re-layouts  160 us (11%)
  blocking collectives  76.8 us (5%)
  other arithmetic  31.6 us (2%)
  between operations  16.6 us (1%)
    reduce_scatter x7, waiting for transfers between devices, per_device(): lax.psum_scatter(partial_value, 'row', scatter_dimension=0, tiled=True)  329 us
    all_gather x7, waiting for transfers between devices, per_device(): lax.all_gather(field, 'row', axis=0, tiled=True)  276 us
    psum x1, waiting for transfers between devices, per_device(): lax.psum((grad_w_input, grad_bias_input, grad_gain_attn, grad_shift_attn,...  152 us
    reduce_scatter x7, waiting for transfers between devices, per_device(): lax.psum_scatter(forward_partial_value, 'col', scatter_dimension=0, tiled...  61.6 us
    dot_general x3, matrix products, node_tail(): projected = jnp.einsum('ntd,de->nte', normed, w_heads, precision=exact)  57.1 us
    psum x1, blocking collectives, per_device(): lax.psum((grad_w_input, grad_bias_input, grad_gain_attn, grad_shift_attn,...  41.8 us
    dot_general x3, matrix products, node_tail(): jnp.einsum('nhqk,nkhe->nqhe', attention, value_rows, precision=exact)  39.7 us
    dot_general x3, matrix products, node_tail(): jnp.einsum('nqhe,nkhe->nhqk', queries, key_rows, precision=exact)  37 us
  transfers between devices with their start and end apart: 22, of which 21 were waited for; matrix products, arithmetic and copies ran while one was open for 5% of the time, Pallas kernels for 0%

commit v1 on v0

--- a/solution.py
+++ b/solution.py
@@ -195,23 +195,26 @@
             partial_value, "row", scatter_dimension=0, tiled=True
         )
     summed = lax.psum(
-        (
-            grad_w_input,
-            grad_bias_input,
-            grad_gain_attn,
-            grad_shift_attn,
-            grad_w_heads,
-            grad_w_merge,
-            grad_bias_merge,
-            grad_gain_ffn,
-            grad_shift_ffn,
-            grad_w_expand,
-            grad_bias_expand,
-            grad_w_reduce,
-            grad_bias_reduce,
-            grad_readout,
+        lax.psum(
+            (
+                grad_w_input,
+                grad_bias_input,
+                grad_gain_attn,
+                grad_shift_attn,
+                grad_w_heads,
+                grad_w_merge,
+                grad_bias_merge,
+                grad_gain_ffn,
+                grad_shift_ffn,
+                grad_w_expand,
+                grad_bias_expand,
+                grad_w_reduce,
+                grad_bias_reduce,
+                grad_readout,
+            ),
+            "col",
         ),
-        ("row", "col"),
+        "row",
     )
     return (
         layer_out,

time: 1410 us -> 1600 us (1.13)
  waiting for transfers between devices: 819 us -> 981 us
  blocking collectives: 76.8 us -> 102 us
    psum x0 -> x1, waiting for transfers between devices: none -> 162 us  [per_device(): lax.psum(lax.psum((grad_w_input, grad_bias_input, grad_gain_attn, grad_sh...]
    psum x0 -> x1, blocking collectives: none -> 60.1 us  [per_device(): lax.psum(lax.psum((grad_w_input, grad_bias_input, grad_gain_attn, grad_sh...]
    psum x1, waiting for transfers between devices: 152 us -> 196 us  [per_device(): lax.psum((grad_w_input, grad_bias_input, grad_gain_attn, grad_shift_attn,...]
    reduce_scatter x7, waiting for transfers between devices: 329 us -> 286 us  [per_device(): lax.psum_scatter(partial_value, 'row', scatter_dimension=0, tiled=True)]
    psum x1, blocking collectives: 41.8 us -> 7.07 us  [per_device(): lax.psum((grad_w_input, grad_bias_input, grad_gain_attn, grad_shift_attn,...]
  transfers between devices with their start and end apart: 22 -> 23, of which waited for: 21 -> 22; matrix products, arithmetic and copies ran while one was open for 5% -> 5% of each run, Pallas kernels for 0% -> 0%
where the time goes in v1:
time: 1600 us; the launch traced here: 1580 us
  waiting for transfers between devices  981 us (61%)
  matrix products  292 us (18%)
  local copies, waits for them, and re-layouts  161 us (10%)
  blocking collectives  102 us (6%)
  other arithmetic  31.6 us (2%)
  between operations  16.4 us (1%)
    reduce_scatter x7, waiting for transfers between devices, per_device(): lax.psum_scatter(partial_value, 'row', scatter_dimension=0, tiled=True)  286 us
    all_gather x7, waiting for transfers between devices, per_device(): lax.all_gather(field, 'row', axis=0, tiled=True)  275 us
    psum x1, waiting for transfers between devices, per_device(): lax.psum((grad_w_input, grad_bias_input, grad_gain_attn, grad_shift_attn,...  196 us
    psum x1, waiting for transfers between devices, per_device(): lax.psum(lax.psum((grad_w_input, grad_bias_input, grad_gain_attn, grad_sh...  162 us
    reduce_scatter x7, waiting for transfers between devices, per_device(): lax.psum_scatter(forward_partial_value, 'col', scatter_dimension=0, tiled...  61.6 us
    psum x1, blocking collectives, per_device(): lax.psum(lax.psum((grad_w_input, grad_bias_input, grad_gain_attn, grad_sh...  60.1 us
    dot_general x3, matrix products, node_tail(): projected = jnp.einsum('ntd,de->nte', normed, w_heads, precision=exact)  57.1 us
    dot_general x3, matrix products, node_tail(): jnp.einsum('nhqk,nkhe->nqhe', attention, value_rows, precision=exact)  39.7 us
  transfers between devices with their start and end apart: 23, of which 22 were waited for; matrix products, arithmetic and copies ran while one was open for 5% of the time, Pallas kernels for 0%

profile of v1, /device:TPU:0, one launch (start us, length us, event | category | flops | bytes accessed | tf_op | source)
XLA Modules:
  0.0 1584.9 jit_solution(1265483429094064749)
XLA Ops:
  9.5 41.4 %all-gather.9.cloned.1.call-done = f32[2048,128]{1,0:T(8,128)} async-done(((f32[128,128]{1,0:T(8,128)}), f32[2048,128]{1,0:T(8,128)}) %all-gather.9.cloned.1.call-update) | async-done | bytes 1048592 | tf_op jit(solution)/shard_map/all_gather | solution.py:101
  59.8 9.3 reduce-scatter.15.cloned.1.call-done
  69.1 40.1 %all-gather.11.cloned.1.call-done = f32[2048,128]{1,0:T(8,128)} async-done(((f32[128,128]{1,0:T(8,128)}), f32[2048,128]{1,0:T(8,128)}) %all-gather.11.cloned.1.call-update) | async-done | bytes 1048592 | tf_op jit(solution)/shard_map/all_gather | solution.py:101
  118.1 9.3 reduce-scatter.17.cloned.1.call-done
  127.4 39.9 %all-gather.13.cloned.1.call-done = f32[2048,128]{1,0:T(8,128)} async-done(((f32[128,128]{1,0:T(8,128)}), f32[2048,128]{1,0:T(8,128)}) %all-gather.13.cloned.1.call-update) | async-done | bytes 1048592 | tf_op jit(solution)/shard_map/all_gather | solution.py:101
  176.1 9.3 reduce-scatter.19.cloned.1.call-done
  185.4 40.1 %all-gather.15.cloned.1.call-done = f32[2048,128]{1,0:T(8,128)} async-done(((f32[128,128]{1,0:T(8,128)}), f32[2048,128]{1,0:T(8,128)}) %all-gather.15.cloned.1.call-update) | async-done | bytes 1048592 | tf_op jit(solution)/shard_map/all_gather | solution.py:101
  234.3 9.3 reduce-scatter.21.cloned.1.call-done
  243.7 40.1 %all-gather.17.cloned.1.call-done = f32[2048,128]{1,0:T(8,128)} async-done(((f32[128,128]{1,0:T(8,128)}), f32[2048,128]{1,0:T(8,128)}) %all-gather.17.cloned.1.call-update) | async-done | bytes 1048592 | tf_op jit(solution)/shard_map/all_gather | solution.py:101
  292.5 9.3 reduce-scatter.23.cloned.1.call-done
  301.9 40.1 %all-gather.19.cloned.1.call-done = f32[2048,128]{1,0:T(8,128)} async-done(((f32[128,128]{1,0:T(8,128)}), f32[2048,128]{1,0:T(8,128)}) %all-gather.19.cloned.1.call-update) | async-done | bytes 1048592 | tf_op jit(solution)/shard_map/all_gather | solution.py:101
  350.7 9.3 reduce-scatter.25.cloned.1.call-done
  366.4 33.8 %all-gather.21.cloned.1.call-done = f32[2048,128]{1,0:T(8,128)} async-done(((f32[128,128]{1,0:T(8,128)}), f32[2048,128]{1,0:T(8,128)}) %all-gather.21.cloned.1.call-update) | async-done | bytes 1048592 | tf_op jit(solution)/shard_map/all_gather | solution.py:101
  412.1 6.1 reduce-scatter.27.cloned.1.call-done
  424.0 10.8 fusion.10
  434.9 14.4 fusion.197
  452.2 5.6 copy.68
  460.8 5.6 copy.67
  469.2 5.6 copy.69
  474.9 9.8 multiply_reduce_fusion.1
  488.9 10.2 convolution_bitcast_fusion.3
  504.3 6.3 fusion.198
  511.2 8.1 fusion.47
  519.3 9.3 fusion.2
  528.7 7.0 add_add_fusion.4
  541.3 6.7 fusion.12
  549.5 14.6 fusion.199
  564.1 7.7 fusion.193
  581.3 5.7 copy.74
  587.1 16.1 %multiply_reduce_fusion = (f32[128,8,8]{2,1,0:T(8,128)}, f32[128,8,8,8]{2,3,1,0:T(8,128)}) fusion(f32[128,8,8]{2,1,0:T(8,128)} %multiply_divide_fusion, f32[128,8,8]{2,1,0:T(8,128)} %copy-done.20, f32[128,8,8,8]{2,3,1,0:T(8,128)} %copy-done.10, f32[128,8,64,8]{2,3,1,0:T(8,128)} %copy.74, f32[128,8,8,64]{3,1,2,0:T(8,128)} %copy.69), kind=kOutput, calls=%fused_computation.25 | convolution fusion | flops 50651136 | bytes 4816896 | tf_op jit(solution)/shard_map/transpose(jvp(nhqk,nkhe->nqhe))/dot_general | solution.py:45
  605.0 12.5 convolution_bitcast_fusion
  617.5 14.7 convolution_bitcast_fusion.1
  632.2 13.5 convolution_bitcast_fusion.2
  660.1 24.2 %fusion.194 = (f32[512]{0:T(512)}, f32[128,8]{0,1:T(8,128)S(1)}, f32[128,8,512]{2,0,1:T(8,128)S(1)}) fusion(f32[512]{0:T(512)S(1)} %copy-done.56, f32[128,8]{0,1:T(8,128)S(1)} %broadcast_multiply_fusion.1, f32[128,8,512]{2,0,1:T(8,128)} %copy-done.3, f32[512]{0:T(512)S(1)} %copy-done.42, f32[512,1536]{1,0:T(8,128)S(1)} %copy-done, ...), kind=kOutput, calls=%fused_computation.282 | convolution fusion | flops 9669965824 | bytes 13645824 | tf_op jit(solution)/shard_map/transpose(jvp(ntd,de->nte))/dot_general | solution.py:37
  705.4 57.5 %reduce-scatter.29.cloned.1.call-done = f32[128,128]{1,0:T(8,128)} async-done(((f32[2048,128]{1,0:T(8,128)}), f32[128,128]{1,0:T(8,128)}) %reduce-scatter.29.cloned.1.call-update) | async-done | bytes 65552 | tf_op jit(solution)/shard_map/reduce_scatter | solution.py:194
  777.7 56.6 %reduce-scatter.31.cloned.1.call-done = f32[128,128]{1,0:T(8,128)} async-done(((f32[2048,128]{1,0:T(8,128)}), f32[128,128]{1,0:T(8,128)}) %reduce-scatter.31.cloned.1.call-update) | async-done | bytes 65552 | tf_op jit(solution)/shard_map/reduce_scatter | solution.py:194
  849.0 56.6 %reduce-scatter.33.cloned.1.call-done = f32[128,128]{1,0:T(8,128)} async-done(((f32[2048,128]{1,0:T(8,128)}), f32[128,128]{1,0:T(8,128)}) %reduce-scatter.33.cloned.1.call-update) | async-done | bytes 65552 | tf_op jit(solution)/shard_map/reduce_scatter | solution.py:194
  920.3 56.5 %reduce-scatter.35.cloned.1.call-done = f32[128,128]{1,0:T(8,128)} async-done(((f32[2048,128]{1,0:T(8,128)}), f32[128,128]{1,0:T(8,128)}) %reduce-scatter.35.cloned.1.call-update) | async-done | bytes 65552 | tf_op jit(solution)/shard_map/reduce_scatter | solution.py:194
  991.9 11.1 fusion.24
  1003.0 45.4 %reduce-scatter.37.cloned.1.call-done = f32[128,128]{1,0:T(8,128)} async-done(((f32[2048,128]{1,0:T(8,128)}), f32[128,128]{1,0:T(8,128)}) %reduce-scatter.37.cloned.1.call-update) | async-done | bytes 65552 | tf_op jit(solution)/shard_map/reduce_scatter | solution.py:194
  1067.4 6.7 convolution_bitcast_fusion.5
  1074.2 10.3 convolution_bitcast_fusion.4
  1084.5 22.1 %fusion.8 = f32[512,1536]{1,0:T(8,128)} fusion(f32[128,8,512]{0,2,1:T(8,128)S(1)} %bitcast.343, f32[128,8,512]{0,2,1:T(8,128)S(1)} %bitcast.341, f32[128,8,512]{0,2,1:T(8,128)S(1)} %bitcast.339, f32[512]{0:T(512)S(1)} %copy-done.70, f32[512]{0:T(512)S(1)} %copy-done.57, f32[128,8]{0,1:T(8,128)S(1)} %copy-done.46, f32[128,8,512]{2,0,1:T(8,128)S(1)} %copy-done.5, ...), kind=kOutput, calls=%fused_computation.42 | convolution fusion | flops 9669443584 | bytes 11548672 | tf_op jit(solution)/shard_map/transpose(jvp(ntd,de->nte))/dot_general | solution.py:37
  1106.7 13.0 reduce-scatter.39.cloned.1.call-done
  1132.8 195.7 %all-reduce.14.cloned.1.call-done = (f32[128,512]{1,0:T(8,128)}, f32[512,1536]{1,0:T(8,128)}, f32[512,512]{1,0:T(8,128)}, f32[512,1024]{1,0:T(8,128)}, f32[1024,512]{1,0:T(8,128)}) async-done(((f32[128,512]{1,0:T(8,128)}, f32[512,1536]{1,0:T(8,128)}, f32[512,512]{1,0:T(8,128)}, f32[512,1024]{1,0:T(8,128)}, f32[1024,512]{1,0:T(8,128)}), (f32[128,512]{1,0:T(8,128)}, f32[512,1536]{1,0:T(8,128)}, ...) | async-done | bytes 8650768 | tf_op jit(solution)/shard_map/psum | solution.py:198
  1331.9 7.1 all-reduce.7
  1338.9 60.1 %all-reduce.5 = (f32[512]{0:T(512)}, f32[512]{0:T(512)}, f32[512]{0:T(512)}, f32[512]{0:T(512)}, f32[512]{0:T(512)}, /*index=5*/f32[512]{0:T(512)}, f32[1024]{0:T(1024)}, f32[512]{0:T(512)}, f32[512]{0:T(512)}) all-reduce(f32[512]{0:T(512)S(1)} %get-tuple-element.40, ...), channel_id=1, replica_groups=mesh['row'=16,'col'=2] {'row'}, use_global_device_ids=true, to_apply=%region_32.0 | all-reduce | flops 5120 | bytes 40960 | tf_op jit(solution)/shard_map/psum | solution.py:197
  1407.1 161.5 %all-reduce.12.cloned.1.call-done = (f32[128,512]{1,0:T(8,128)}, f32[512,1536]{1,0:T(8,128)}, f32[512,512]{1,0:T(8,128)}, f32[512,1024]{1,0:T(8,128)}, f32[1024,512]{1,0:T(8,128)}) async-done(((f32[128,512]{1,0:T(8,128)}, f32[512,1536]{1,0:T(8,128)}, f32[512,512]{1,0:T(8,128)}, f32[512,1024]{1,0:T(8,128)}, f32[1024,512]{1,0:T(8,128)}), (f32[128,512]{1,0:T(8,128)}, f32[512,1536]{1,0:T(8,128)}, ...) | async-done | bytes 8650768 | tf_op jit(solution)/shard_map/psum | solution.py:197
  (335 shorter events, 262.7 us)
Async XLA Ops:
  7.2 416.8 %copy-start = (f32[512,1536]{1,0:T(8,128)S(1)}, f32[512,1536]{1,0:T(8,128)}, u32[]{:S(2)}) copy-start(f32[512,1536]{1,0:T(8,128)} %param.29) | copy-start | bytes 9437188
  7.2 162.6 %copy-start.6 = (f32[1,1,4,128,128]{4,3,2,1,0:T(8,128)S(1)}, f32[1,1,4,128,128]{4,3,2,1,0:T(8,128)}, u32[]{:S(2)}) copy-start(f32[1,1,4,128,128]{4,3,2,1,0:T(8,128)} %param.21) | copy-start | bytes 786436
  7.2 108.6 %copy-start.52 = (s32[1,1,4]{2,1,0:T(1,128)S(1)}, s32[1,1,4]{2,1,0:T(1,128)}, u32[]{:S(2)}) copy-start(s32[1,1,4]{2,1,0:T(1,128)} %param.22) | copy-start | bytes 52
  7.2 43.7 %all-gather.9.cloned.1.call-start = ((), (), s32[]{:S(2)}) async-start(), calls=%async_computation.14 | async-start | bytes 1114112 | tf_op jit(solution)/shard_map/all_gather | solution.py:101
  8.0 61.1 %reduce-scatter.15.cloned.1.call-start = ((), (), s32[]{:S(2)}) async-start(), calls=%async_computation.15 | async-start | bytes 196608 | tf_op jit(solution)/shard_map/reduce_scatter | solution.py:110
  59.7 49.5 %all-gather.11.cloned.1.call-start = ((), (), s32[]{:S(2)}) async-start(), calls=%async_computation.16 | async-start | bytes 1114112 | tf_op jit(solution)/shard_map/all_gather | solution.py:101
  69.1 58.3 %reduce-scatter.17.cloned.1.call-start = ((), (), s32[]{:S(2)}) async-start(), calls=%async_computation.17 | async-start | bytes 196608 | tf_op jit(solution)/shard_map/reduce_scatter | solution.py:110
  118.0 49.3 %all-gather.13.cloned.1.call-start = ((), (), s32[]{:S(2)}) async-start(), calls=%async_computation.18 | async-start | bytes 1114112 | tf_op jit(solution)/shard_map/all_gather | solution.py:101
  127.3 58.0 %reduce-scatter.19.cloned.1.call-start = ((), (), s32[]{:S(2)}) async-start(), calls=%async_computation.19 | async-start | bytes 196608 | tf_op jit(solution)/shard_map/reduce_scatter | solution.py:110
  176.0 184.7 %copy-start.40 = (f32[128,128]{1,0:T(8,128)S(1)}, f32[128,128]{1,0:T(8,128)}, u32[]{:S(2)}) copy-start(f32[128,128]{1,0:T(8,128)} %param.20) | copy-start | bytes 196612
  176.0 185.3 %copy-start.41 = (f32[128,128]{1,0:T(8,128)S(1)}, f32[128,128]{1,0:T(8,128)}, u32[]{:S(2)}) copy-start(f32[128,128]{1,0:T(8,128)} %reduce-scatter.15.cloned.1.call-done) | copy-start | bytes 196612
  176.1 49.5 %all-gather.15.cloned.1.call-start = ((), (), s32[]{:S(2)}) async-start(), calls=%async_computation.20 | async-start | bytes 1114112 | tf_op jit(solution)/shard_map/all_gather | solution.py:101
  185.4 58.2 %reduce-scatter.21.cloned.1.call-start = ((), (), s32[]{:S(2)}) async-start(), calls=%async_computation.21 | async-start | bytes 196608 | tf_op jit(solution)/shard_map/reduce_scatter | solution.py:110
  234.3 49.5 %all-gather.17.cloned.1.call-start = ((), (), s32[]{:S(2)}) async-start(), calls=%async_computation.22 | async-start | bytes 1114112 | tf_op jit(solution)/shard_map/all_gather | solution.py:101
  243.6 58.2 %reduce-scatter.23.cloned.1.call-start = ((), (), s32[]{:S(2)}) async-start(), calls=%async_computation.23 | async-start | bytes 196608 | tf_op jit(solution)/shard_map/reduce_scatter | solution.py:110
  286.2 133.5 %copy-start.42 = (f32[512]{0:T(512)S(1)}, f32[512]{0:T(512)}, u32[]{:S(2)}) copy-start(f32[512]{0:T(512)} %param.26) | copy-start | bytes 6148
  292.5 49.5 %all-gather.19.cloned.1.call-start = ((), (), s32[]{:S(2)}) async-start(), calls=%async_computation.24 | async-start | bytes 1114112 | tf_op jit(solution)/shard_map/all_gather | solution.py:101
  301.8 58.2 %reduce-scatter.25.cloned.1.call-start = ((), (), s32[]{:S(2)}) async-start(), calls=%async_computation.25 | async-start | bytes 196608 | tf_op jit(solution)/shard_map/reduce_scatter | solution.py:110
  350.7 49.5 %all-gather.21.cloned.1.call-start = ((), (), s32[]{:S(2)}) async-start(), calls=%async_computation.26 | async-start | bytes 1114112 | tf_op jit(solution)/shard_map/all_gather | solution.py:101
  360.0 58.2 %reduce-scatter.27.cloned.1.call-start = ((), (), s32[]{:S(2)}) async-start(), calls=%async_computation.27 | async-start | bytes 196608 | tf_op jit(solution)/shard_map/reduce_scatter | solution.py:110
  362.0 62.1 %copy-start.56 = (f32[512]{0:T(512)S(1)}, f32[512]{0:T(512)}, u32[]{:S(2)}) copy-start(f32[512]{0:T(512)} %param.27) | copy-start | bytes 6148
  362.0 62.1 %copy-start.69 = (f32[512]{0:T(512)S(1)}, f32[512]{0:T(512)}, u32[]{:S(2)}) copy-start(f32[512]{0:T(512)} %param.28) | copy-start | bytes 6148
  408.9 354.1 %reduce-scatter.29.cloned.1.call-start = ((), (), s32[]{:S(2)}) async-start(), calls=%async_computation.28 | async-start | bytes 1114112 | tf_op jit(solution)/shard_map/reduce_scatter | solution.py:194
  424.0 262.1 %copy-start.45 = (f32[128,8]{0,1:T(8,128)}, f32[128,8]{0,1:T(8,128)S(1)}, u32[]{:S(2)}) copy-start(f32[128,8]{0,1:T(8,128)S(1)} %fusion.126) | copy-start | bytes 12292
  510.7 17.9 %copy-start.1 = (f32[128,8,512]{2,0,1:T(8,128)}, f32[128,8,512]{2,0,1:T(8,128)S(1)}, u32[]{:S(2)}) copy-start(f32[128,8,512]{2,0,1:T(8,128)S(1)} %get-tuple-element.69) | copy-start | bytes 6291460
  511.2 62.4 %copy-start.47 = (f32[128,8]{0,1:T(8,128)}, f32[128,8]{0,1:T(8,128)S(1)}, u32[]{:S(2)}) copy-start(f32[128,8]{0,1:T(8,128)S(1)} %fusion.127) | copy-start | bytes 12292
  548.1 15.9 %copy-start.48 = (f32[128,7]{0,1:T(8,128)}, f32[128,7]{0,1:T(8,128)S(1)}, u32[]{:S(2)}) copy-start(f32[128,7]{0,1:T(8,128)S(1)} %get-tuple-element.63) | copy-start | bytes 10756
  548.2 15.9 %copy-start.50 = (f32[128,7]{0,1:T(8,128)}, f32[128,7]{0,1:T(8,128)S(1)}, u32[]{:S(2)}) copy-start(f32[128,7]{0,1:T(8,128)S(1)} %get-tuple-element.62) | copy-start | bytes 10756
  549.4 24.1 %copy-start.18 = (f32[128,7,512]{2,0,1:T(8,128)}, f32[128,7,512]{2,0,1:T(8,128)S(1)}, u32[]{:S(2)}) copy-start(f32[128,7,512]{2,0,1:T(8,128)S(1)} %multiply_add_fusion.3) | copy-start | bytes 5505028
  549.4 14.7 copy-start.2
  549.5 14.6 copy-start.36
  587.0 18.0 %copy-start.11 = (f32[128,8,8,8]{2,3,1,0:T(8,128)S(1)}, f32[128,8,8,8]{2,3,1,0:T(8,128)}, u32[]{:S(2)}) copy-start(f32[128,8,8,8]{2,3,1,0:T(8,128)} %copy-done.10) | copy-start | bytes 786436
  587.0 18.0 %copy-start.16 = (f32[128,8,8,64]{3,1,2,0:T(8,128)S(1)}, f32[128,8,8,64]{3,1,2,0:T(8,128)}, u32[]{:S(2)}) copy-start(f32[128,8,8,64]{3,1,2,0:T(8,128)} %copy.68) | copy-start | bytes 6291460
  587.1 18.0 %copy-start.21 = (f32[128,8,8]{2,1,0:T(8,128)S(1)}, f32[128,8,8]{2,1,0:T(8,128)}, u32[]{:S(2)}) copy-start(f32[128,8,8]{2,1,0:T(8,128)} %copy-done.20) | copy-start | bytes 98308
  587.1 18.0 %copy-start.30 = (f32[128,8,8]{2,1,0:T(8,128)S(1)}, f32[128,8,8]{2,1,0:T(8,128)}, u32[]{:S(2)}) copy-start(f32[128,8,8]{2,1,0:T(8,128)} %copy-done.29) | copy-start | bytes 98308
  660.0 24.3 %copy-start.4 = (f32[128,8,512]{2,0,1:T(8,128)S(1)}, f32[128,8,512]{2,0,1:T(8,128)}, u32[]{:S(2)}) copy-start(f32[128,8,512]{2,0,1:T(8,128)} %copy-done.3) | copy-start | bytes 6291460
  705.4 128.9 %reduce-scatter.31.cloned.1.call-start = ((), (), s32[]{:S(2)}) async-start(), calls=%async_computation.29 | async-start | bytes 1114112 | tf_op jit(solution)/shard_map/reduce_scatter | solution.py:194
  777.7 127.9 %reduce-scatter.33.cloned.1.call-start = ((), (), s32[]{:S(2)}) async-start(), calls=%async_computation.30 | async-start | bytes 1114112 | tf_op jit(solution)/shard_map/reduce_scatter | solution.py:194
  849.0 127.8 %reduce-scatter.35.cloned.1.call-start = ((), (), s32[]{:S(2)}) async-start(), calls=%async_computation.31 | async-start | bytes 1114112 | tf_op jit(solution)/shard_map/reduce_scatter | solution.py:194
  920.3 128.2 %reduce-scatter.37.cloned.1.call-start = ((), (), s32[]{:S(2)}) async-start(), calls=%async_computation.32 | async-start | bytes 1114112 | tf_op jit(solution)/shard_map/reduce_scatter | solution.py:194
  991.9 127.8 %reduce-scatter.39.cloned.1.call-start = ((), (), s32[]{:S(2)}) async-start(), calls=%async_computation.33 | async-start | bytes 1114112 | tf_op jit(solution)/shard_map/reduce_scatter | solution.py:194
  1063.1 11.0 copy-start.44
  1063.1 265.4 %all-reduce.14.cloned.1.call-start = ((), (), s32[]{:S(2)}) async-start(), calls=%async_computation.36 | async-start | bytes 17301504 | tf_op jit(solution)/shard_map/psum | solution.py:198
  1063.4 10.8 copy-start.8
  1063.4 10.7 copy-start.19
  1106.6 23.7 %copy-start.53 = (s32[1,1,4]{2,1,0:T(1,128)S(1)}, s32[1,1,4]{2,1,0:T(1,128)}, u32[]{:S(2)}) copy-start(s32[1,1,4]{2,1,0:T(1,128)} %param.23) | copy-start | bytes 52
  1106.6 298.9 %reduce-scatter.41.cloned.1.call-start = ((), (), s32[]{:S(2)}) async-start(), calls=%async_computation.34 | async-start | bytes 1114112 | tf_op jit(solution)/shard_map/reduce_scatter | solution.py:194
  1132.7 435.9 %all-reduce.12.cloned.1.call-start = ((), (), s32[]{:S(2)}) async-start(), calls=%async_computation.35 | async-start | bytes 17301504 | tf_op jit(solution)/shard_map/psum | solution.py:197
  (46 other events, 235.6 us)
Sparse Core Ops, SparseCore 0:
  10.2 40.6 all-gather.8
  59.8 9.1 reduce-scatter.14
  71.2 37.9 all-gather.10
  118.1 9.1 reduce-scatter.16
  129.3 37.9 all-gather.12
  176.2 9.1 reduce-scatter.18
  187.5 37.9 all-gather.14
  234.4 9.1 reduce-scatter.20
  245.7 37.9 all-gather.16
  292.6 9.1 reduce-scatter.22
  304.0 37.9 all-gather.18
  350.8 9.1 reduce-scatter.24
  362.2 37.9 all-gather.20
  409.0 9.1 reduce-scatter.26
  705.5 57.4 reduce-scatter.28
  777.8 56.4 reduce-scatter.30
  849.1 56.4 reduce-scatter.32
  920.4 56.3 reduce-scatter.34
  992.0 56.4 reduce-scatter.36
  1063.3 56.3 reduce-scatter.38
  1123.7 204.7 all-reduce.13
  1332.7 57.4 reduce-scatter.40
  1395.0 173.5 all-reduce.11
